TPU v7x, 128 devices: a whole 4x4x4 slice. The times are simulated.
128 devices in a mesh: fsdp: 32 (over z_lo, x, y), dp: 4 (over z_hi, core).
Axes of the slice: x: 4, y: 4, z: 4 (z_hi: 2, z_lo: 2; z = z_hi * 2 + z_lo), core: 2. Of those that a mesh axis runs over, the one named last changes fastest.
Arguments:
- teacher_hidden: bfloat16 [1024, 8192], P(('fsdp', 'dp'))
- student_hidden: bfloat16 [1024, 4096], P(('fsdp', 'dp'))
- teacher_head: bfloat16 [8192, 65536], P('dp', 'fsdp'), may hold values from -0.1875 to 0.1875
- student_head: bfloat16 [4096, 65536], P('dp', 'fsdp'), may hold values from -0.25 to 0.25
- actions: int32 [1024], replicated, may hold values from 0 to 65535
- advantages: float32 [1024], replicated, may hold values from -0.21875 to 0.21875
- loss_mask: int32 [1024], replicated, may hold values 0 or 1
Outputs:
- token_loss: float32 [1024], P('dp')
- head_grad: float32 [4096, 65536], P('dp', 'fsdp')
- hidden_grad: bfloat16 [1024, 4096], P('fsdp', 'dp')
All inputs are finite; a program needn't handle non-finite values.
Results may differ from a plain program's by a relative error of at most 0.0048.
Values may be sent and summed in bfloat16 or wider, within the bound.
No kernel may reach another device: no remote copies, remote signals or barrier semaphores. Data moves between devices by JAX's collectives and lax.ppermute only.
A program may use at most 128 MiB of HBM per device.

v0:
```python
import jax
import jax.numpy as jnp
from jax import lax
from jax.sharding import PartitionSpec as P

kl_weight = 0.5


def shards(
    teacher_hidden, student_hidden, teacher_head, student_head, actions, advantages, loss_mask
):
    teacher_part, student_part = (
        lax.all_to_all(teacher_hidden, "dp", split_axis=1, concat_axis=0, tiled=True),
        lax.all_to_all(student_hidden, "dp", split_axis=1, concat_axis=0, tiled=True),
    )
    teacher_rows, student_rows = (
        lax.all_gather(teacher_part, "fsdp", axis=0, tiled=True),
        lax.all_gather(student_part, "fsdp", axis=0, tiled=True),
    )
    total_rows = teacher_rows.shape[0]
    share = total_rows // lax.axis_size("dp")
    teacher_partial = jnp.dot(teacher_rows, teacher_head, preferred_element_type=jnp.float32)
    student_partial = jnp.dot(student_rows, student_head, preferred_element_type=jnp.float32)
    teacher_logits, student_logits = (
        lax.psum_scatter(teacher_partial, "dp", scatter_dimension=0, tiled=True),
        lax.psum_scatter(student_partial, "dp", scatter_dimension=0, tiled=True),
    )
    first_row = lax.axis_index("dp") * share
    chosen = lax.dynamic_slice_in_dim(actions, first_row, share)
    benefit = lax.dynamic_slice_in_dim(advantages, first_row, share)
    weight = lax.dynamic_slice_in_dim(loss_mask, first_row, share).astype(jnp.float32)
    vocab_shard = teacher_logits.shape[1]
    columns = lax.axis_index("fsdp") * vocab_shard + jnp.arange(vocab_shard, dtype=jnp.int32)
    onehot = (chosen[:, None] == columns[None, :]).astype(jnp.float32)
    local_pick = jnp.sum(onehot * student_logits, axis=1)
    teacher_max, student_max = lax.pmax(
        (jnp.max(teacher_logits, axis=1), jnp.max(student_logits, axis=1)), "fsdp"
    )
    teacher_exp = jnp.exp(teacher_logits - teacher_max[:, None])
    student_exp = jnp.exp(student_logits - student_max[:, None])
    teacher_sum, student_sum, cross, pick = lax.psum(
        (
            jnp.sum(teacher_exp, axis=1),
            jnp.sum(student_exp, axis=1),
            jnp.sum(teacher_exp * (teacher_logits - student_logits), axis=1),
            local_pick,
        ),
        "fsdp",
    )
    teacher_lse = teacher_max + jnp.log(teacher_sum)
    student_lse = student_max + jnp.log(student_sum)
    kl = cross / teacher_sum - teacher_lse + student_lse
    action_logp = pick - student_lse
    losses = weight * (kl_weight * kl - benefit * action_logp)
    teacher_prob = teacher_exp / teacher_sum[:, None]
    student_prob = student_exp / student_sum[:, None]
    logit_grad = (
        weight[:, None]
        * (kl_weight * (student_prob - teacher_prob) + benefit[:, None] * (student_prob - onehot))
    ).astype(jnp.bfloat16)
    grad_all = lax.all_gather(logit_grad, "dp", axis=0, tiled=True)
    head_grad = lax.dot_general(
        student_rows, grad_all, (((0,), (0,)), ((), ())), preferred_element_type=jnp.float32
    )
    hidden_grad = lax.psum_scatter(
        lax.dot_general(
            grad_all, student_head, (((1,), (1,)), ((), ())), preferred_element_type=jnp.float32
        ),
        "fsdp",
        scatter_dimension=0,
        tiled=True,
    ).astype(jnp.bfloat16)
    return (losses, head_grad, hidden_grad)


def solution(mesh):
    placed = (
        P(("fsdp", "dp"), None),
        P(("fsdp", "dp"), None),
        P("dp", "fsdp"),
        P("dp", "fsdp"),
        P(),
        P(),
        P(),
    )
    return jax.shard_map(
        shards,
        mesh=mesh,
        in_specs=placed,
        out_specs=(P("dp"), P("dp", "fsdp"), P("fsdp", "dp")),
        check_vma=False,
    )
```

profile of v0, /device:TPU:0, one launch (start us, length us, event | category | flops | bytes accessed | tf_op | source)
XLA Modules:
  0.0 882.2 jit_solution(9315248481486084040)
XLA Ops:
  7.2 0.0 all-gather.6.cloned.1.call-start
  7.2 11.0 %all_to_all.38 = bf16[8,4,1024]{2,0,1:T(8,128)(2,1)} all-to-all(bf16[8,4,1024]{2,0,1:T(8,128)(2,1)} %bitcast.21), channel_id=1, replica_groups=mesh['fsdp'=32,'dp'=4] {'dp'}, dimensions={1} | all-to-all | bytes 131072 | tf_op jit(solution)/shard_map/all_to_all | solution.py:14
  18.2 0.0 all-gather.6.cloned.1.call-update
  18.2 0.0 all-gather.4.cloned.1.call-start
  18.3 10.1 %all_to_all.39 = bf16[8,4,2048]{2,0,1:T(8,128)(2,1)} all-to-all(bf16[8,4,2048]{2,0,1:T(8,128)(2,1)} %bitcast.20), channel_id=1, replica_groups=mesh['fsdp'=32,'dp'=4] {'dp'}, dimensions={1} | all-to-all | bytes 262144 | tf_op jit(solution)/shard_map/all_to_all | solution.py:13
  28.4 0.0 all-gather.4.cloned.1.call-update
  28.4 0.0 reduce-scatter.6.cloned.1.call-start
  28.5 141.8 %all-gather.6.cloned.1.call-done = bf16[1024,1024]{1,0:T(8,128)(2,1)} async-done(((bf16[32,1024]{1,0:T(8,128)(2,1)}), bf16[1024,1024]{1,0:T(8,128)(2,1)}) %all-gather.6.cloned.1.call-update) | async-done | bytes 2097168 | tf_op jit(solution)/shard_map/all_gather | solution.py:18
  170.3 10.5 %fusion.9 = f32[1024,2048]{1,0:T(8,128)} fusion(bf16[1024,1024]{1,0:T(8,128)(2,1)} %all-gather.6.cloned.1.call-done, bf16[1024,2048]{1,0:T(8,128)(2,1)} %param.10), kind=kOutput, calls=%fused_computation.18 | convolution fusion | flops 4294967296 | bytes 14680064 | tf_op jit(solution)/shard_map/dot_general | solution.py:23
  180.8 0.0 reduce-scatter.6.cloned.1.call-update
  180.8 0.0 reduce-scatter.4.cloned.1.call-start
  180.9 147.8 %all-gather.4.cloned.1.call-done = bf16[1024,2048]{1,0:T(8,128)(2,1)} async-done(((bf16[32,2048]{1,0:T(8,128)(2,1)}), bf16[1024,2048]{1,0:T(8,128)(2,1)}) %all-gather.4.cloned.1.call-update) | async-done | bytes 4194320 | tf_op jit(solution)/shard_map/all_gather | solution.py:17
  328.7 14.8 %fusion.8 = f32[1024,2048]{1,0:T(8,128)} fusion(bf16[1024,2048]{1,0:T(8,128)(2,1)} %all-gather.4.cloned.1.call-done, bf16[2048,2048]{1,0:T(8,128)(2,1)} %param.9), kind=kOutput, calls=%fused_computation.17 | convolution fusion | flops 8589934592 | bytes 20971520 | tf_op jit(solution)/shard_map/dot_general | solution.py:22
  343.4 0.0 reduce-scatter.4.cloned.1.call-update
  343.4 0.0 all-gather.8.cloned.1.call-start
  343.5 0.8 dynamic_slice.11
  344.3 66.0 %reduce-scatter.6.cloned.1.call-done = f32[256,2048]{1,0:T(8,128)} async-done(((f32[1024,2048]{1,0:T(8,128)}), f32[256,2048]{1,0:T(8,128)}) %reduce-scatter.6.cloned.1.call-update) | async-done | bytes 2097168 | tf_op jit(solution)/shard_map/reduce_scatter | solution.py:26
  410.3 0.0 copy-start
  410.3 1.9 reduce_max.19
  412.2 78.9 %reduce-scatter.4.cloned.1.call-done = f32[256,2048]{1,0:T(8,128)} async-done(((f32[1024,2048]{1,0:T(8,128)}), f32[256,2048]{1,0:T(8,128)}) %reduce-scatter.4.cloned.1.call-update) | async-done | bytes 2097168 | tf_op jit(solution)/shard_map/reduce_scatter | solution.py:25
  491.1 1.8 reduce_max.18
  492.9 81.8 %all-reduce.1 = (f32[256]{0:T(256)S(1)}, f32[256]{0:T(256)S(1)}) all-reduce(f32[256]{0:T(256)S(1)} %reduce_max.18, f32[256]{0:T(256)S(1)} %reduce_max.19), channel_id=1, replica_groups=mesh['fsdp'=32,'dp'=4] {'fsdp'}, use_global_device_ids=true, to_apply=%region_2.0 | all-reduce | flops 512 | bytes 4096 | tf_op jit(solution)/shard_map/pmax | solution.py:36
  574.6 0.0 copy-done
  574.7 2.8 multiply_reduce_fusion
  577.5 76.8 %all-reduce = (f32[256]{0:T(256)S(1)}, f32[256]{0:T(256)S(1)}, f32[256]{0:T(256)S(1)}, f32[256]{0:T(256)S(1)}) all-reduce(f32[256]{0:T(256)S(1)} %get-tuple-element.8, f32[256]{0:T(256)S(1)} %get-tuple-element.9, f32[256]{0:T(256)S(1)} %get-tuple-element.7, f32[256]{0:T(256)S(1)} %get-tuple-element.6), channel_id=1, replica_groups=mesh['fsdp'=32,'dp'=4] {'fsdp'}, use_global_device_ids=true, to_apply=%region_13.0 | all-reduce | flops 1024 | bytes 8192 | tf_op jit(solution)/shard_map/psum | solution.py:41
  654.3 1.3 subtract_multiply_fusion
  655.7 3.4 fusion.5
  659.1 0.0 all-gather.8.cloned.1.call-update
  659.1 0.2 reduce-scatter.8.cloned.1.call-start
  659.4 35.1 %all-gather.8.cloned.1.call-done = bf16[1024,2048]{1,0:T(8,128)(2,1)} async-done(((bf16[256,2048]{1,0:T(8,128)(2,1)}), bf16[1024,2048]{1,0:T(8,128)(2,1)}) %all-gather.8.cloned.1.call-update) | async-done | bytes 4194320 | tf_op jit(solution)/shard_map/all_gather | solution.py:61
  694.5 10.0 %fusion.10 = f32[1024,1024]{1,0:T(8,128)} fusion(bf16[1024,2048]{1,0:T(8,128)(2,1)} %all-gather.8.cloned.1.call-done, bf16[1024,2048]{1,0:T(8,128)(2,1)} %param.10), kind=kOutput, calls=%fused_computation.19 | convolution fusion | flops 4294967296 | bytes 12582912 | tf_op jit(solution)/shard_map/dot_general | solution.py:66
  704.5 0.0 copy-start.1
  704.5 0.0 reduce-scatter.8.cloned.1.call-update
  704.5 1.6 copy-done.1
  706.1 9.0 %convolution_bitcast_fusion = f32[1024,2048]{0,1:T(8,128)} fusion(bf16[1024,2048]{1,0:T(8,128)(2,1)} %all-gather.8.cloned.1.call-done, bf16[1024,1024]{1,0:T(8,128)(2,1)S(1)} %copy-done.1), kind=kOutput, calls=%fused_computation | convolution fusion | flops 4294967296 | bytes 14680064 | tf_op jit(solution)/shard_map/dot_general | solution.py:62
  715.1 9.1 %copy.10 = f32[1024,2048]{1,0:T(8,128)} copy(f32[1024,2048]{0,1:T(8,128)} %convolution_bitcast_fusion) | data formatting | bytes 16777216
  724.2 149.6 %reduce-scatter.8.cloned.1.call-done = f32[32,1024]{1,0:T(8,128)} async-done(((f32[1024,1024]{1,0:T(8,128)}), f32[32,1024]{1,0:T(8,128)}) %reduce-scatter.8.cloned.1.call-update) | async-done | bytes 131088 | tf_op jit(solution)/shard_map/reduce_scatter | solution.py:65
  873.8 1.5 convert_element_type.15
  (1 shorter events, 0.0 us)
Async XLA Ops:
  7.2 163.1 %all-gather.6.cloned.1.call-start = ((), (), s32[]{:S(2)}) async-start(), calls=%async_computation.7 | async-start | bytes 2162688 | tf_op jit(solution)/shard_map/all_gather | solution.py:18
  18.2 310.4 %all-gather.4.cloned.1.call-start = ((), (), s32[]{:S(2)}) async-start(), calls=%async_computation.5 | async-start | bytes 4325376 | tf_op jit(solution)/shard_map/all_gather | solution.py:17
  28.4 381.9 %reduce-scatter.6.cloned.1.call-start = ((), (), s32[]{:S(2)}) async-start(), calls=%async_computation.8 | async-start | bytes 10485760 | tf_op jit(solution)/shard_map/reduce_scatter | solution.py:26
  180.8 310.3 %reduce-scatter.4.cloned.1.call-start = ((), (), s32[]{:S(2)}) async-start(), calls=%async_computation.6 | async-start | bytes 10485760 | tf_op jit(solution)/shard_map/reduce_scatter | solution.py:25
  343.4 351.1 %all-gather.8.cloned.1.call-start = ((), (), s32[]{:S(2)}) async-start(), calls=%async_computation.9 | async-start | bytes 5242880 | tf_op jit(solution)/shard_map/all_gather | solution.py:61
  410.3 164.4 %copy-start = (f32[256,2048]{1,0:T(8,128)S(1)}, f32[256,2048]{1,0:T(8,128)}, u32[]{:S(2)}) copy-start(f32[256,2048]{1,0:T(8,128)} %reduce-scatter.6.cloned.1.call-done) | copy-start | bytes 6291460
  659.1 214.7 %reduce-scatter.8.cloned.1.call-start = ((), (), s32[]{:S(2)}) async-start(), calls=%async_computation.10 | async-start | bytes 4325376 | tf_op jit(solution)/shard_map/reduce_scatter | solution.py:65
  704.5 1.6 copy-start.1
Sparse Core Ops, SparseCore 0:
  18.4 151.8 all-gather.5
  171.9 156.6 all-gather.3
  331.3 78.8 reduce-scatter.5
  413.4 77.6 reduce-scatter.3
  659.3 35.1 all-gather.7
  704.6 169.1 reduce-scatter.7
where the time goes:
time: 883 us; the launch traced here: 882 us
  waiting for transfers between devices  619 us (70%)
  blocking collectives  180 us (20%)
  matrix products  44.3 us (5%)
  between operations  14.1 us (2%)
  other arithmetic  12.9 us (1%)
  local copies, waits for them, and re-layouts  11.5 us (1%)
    reduce_scatter x1, waiting for transfers between devices, shards(): lax.psum_scatter(lax.dot_general(grad_all, student_head, (((1,), (1,)), (...  150 us
    all_gather x1, waiting for transfers between devices, shards(): lax.all_gather(teacher_part, 'fsdp', axis=0, tiled=True)  148 us
    all_gather x1, waiting for transfers between devices, shards(): lax.all_gather(student_part, 'fsdp', axis=0, tiled=True)  142 us
    pmax x1, blocking collectives, shards(): lax.pmax((jnp.max(teacher_logits, axis=1), jnp.max(student_logits, axis=1...  81.8 us
    reduce_scatter x1, waiting for transfers between devices, shards(): lax.psum_scatter(teacher_partial, 'dp', scatter_dimension=0, tiled=True)  78.9 us
    psum x1, blocking collectives, shards(): lax.psum((jnp.sum(teacher_exp, axis=1), jnp.sum(student_exp, axis=1), jnp...  76.8 us
    reduce_scatter x1, waiting for transfers between devices, shards(): lax.psum_scatter(student_partial, 'dp', scatter_dimension=0, tiled=True)  66 us
    all_gather x1, waiting for transfers between devices, shards(): grad_all = lax.all_gather(logit_grad, 'dp', axis=0, tiled=True)  35.1 us
  transfers between devices with their start and end apart: 6, of which 6 were waited for; matrix products, arithmetic and copies ran while one was open for 5% of the time, Pallas kernels for 0%

commit v1 on v0

--- a/solution.py
+++ b/solution.py
@@ -13,9 +13,16 @@
         lax.all_to_all(teacher_hidden, "dp", split_axis=1, concat_axis=0, tiled=True),
         lax.all_to_all(student_hidden, "dp", split_axis=1, concat_axis=0, tiled=True),
     )
+
+    def series_pair(values):
+        return jnp.concatenate(
+            lax.all_to_all(jnp.stack(lax.axis_size("fsdp") * [values], axis=0), "fsdp", 0, 0),
+            axis=0,
+        )
+
     teacher_rows, student_rows = (
         lax.all_gather(teacher_part, "fsdp", axis=0, tiled=True),
-        lax.all_gather(student_part, "fsdp", axis=0, tiled=True),
+        series_pair(student_part),
     )
     total_rows = teacher_rows.shape[0]
     share = total_rows // lax.axis_size("dp")

time: 883 us -> 674 us (0.76)
  waiting for transfers between devices: 619 us -> 371 us
  blocking collectives: 180 us -> 220 us
    all_gather x1 -> x0, waiting for transfers between devices: 142 us -> none  [shards(): lax.all_gather(student_part, 'fsdp', axis=0, tiled=True)]
    reduce_scatter x1, waiting for transfers between devices: 66 us -> 0.01 us  [shards(): lax.psum_scatter(student_partial, 'dp', scatter_dimension=0, tiled=True)]
    all_to_all x0 -> x1, blocking collectives: none -> 40.7 us  [series_pair(): lax.all_to_all(jnp.stack(lax.axis_size('fsdp') * [values], axis=0), 'fsdp...]
    all_gather x1, waiting for transfers between devices: 148 us -> 113 us  [shards(): lax.all_gather(teacher_part, 'fsdp', axis=0, tiled=True)]
  transfers between devices with their start and end apart: 6 -> 5, of which waited for: 6 -> 4; matrix products, arithmetic and copies ran while one was open for 5% -> 6% of each run, Pallas kernels for 0% -> 0%
where the time goes in v1:
time: 674 us; the launch traced here: 673 us
  waiting for transfers between devices  371 us (55%)
  blocking collectives  220 us (33%)
  matrix products  40.1 us (6%)
  between operations  15.7 us (2%)
  local copies, waits for them, and re-layouts  13.1 us (2%)
  other arithmetic  12.9 us (2%)
    reduce_scatter x1, waiting for transfers between devices, shards(): lax.psum_scatter(lax.dot_general(grad_all, student_head, (((1,), (1,)), (...  149 us
    all_gather x1, waiting for transfers between devices, shards(): lax.all_gather(teacher_part, 'fsdp', axis=0, tiled=True)  113 us
    pmax x1, blocking collectives, shards(): lax.pmax((jnp.max(teacher_logits, axis=1), jnp.max(student_logits, axis=1...  81.8 us
    psum x1, blocking collectives, shards(): lax.psum((jnp.sum(teacher_exp, axis=1), jnp.sum(student_exp, axis=1), jnp...  76.8 us
    reduce_scatter x1, waiting for transfers between devices, shards(): lax.psum_scatter(teacher_partial, 'dp', scatter_dimension=0, tiled=True)  73.8 us
    all_to_all x1, blocking collectives, series_pair(): lax.all_to_all(jnp.stack(lax.axis_size('fsdp') * [values], axis=0), 'fsdp...  40.7 us
    all_gather x1, waiting for transfers between devices, shards(): grad_all = lax.all_gather(logit_grad, 'dp', axis=0, tiled=True)  35 us
    dot_general x1, matrix products, shards(): jnp.dot(teacher_rows, teacher_head, preferred_element_type=jnp.float32)  14.5 us
  transfers between devices with their start and end apart: 5, of which 4 were waited for; matrix products, arithmetic and copies ran while one was open for 6% of the time, Pallas kernels for 0%

profile of v1, /device:TPU:0, one launch (start us, length us, event | category | flops | bytes accessed | tf_op | source)
XLA Modules:
  0.0 673.0 jit_solution(659979728416328940)
XLA Ops:
  8.0 0.0 all-gather.3.cloned.1.call-start
  8.0 11.5 %all_to_all.40 = bf16[8,4,2048]{2,0,1:T(8,128)(2,1)} all-to-all(bf16[8,4,2048]{2,0,1:T(8,128)(2,1)} %bitcast.23), channel_id=1, replica_groups=mesh['fsdp'=32,'dp'=4] {'dp'}, dimensions={1} | all-to-all | bytes 262144 | tf_op jit(solution)/shard_map/all_to_all | solution.py:13
  19.5 0.0 all-gather.3.cloned.1.call-update
  19.5 0.0 reduce-scatter.6.cloned.1.call-start
  19.6 8.9 %all_to_all.41 = bf16[8,4,1024]{2,0,1:T(8,128)(2,1)S(1)} all-to-all(bf16[8,4,1024]{2,0,1:T(8,128)(2,1)} %bitcast.24), channel_id=1, replica_groups=mesh['fsdp'=32,'dp'=4] {'dp'}, dimensions={1} | all-to-all | bytes 131072 | tf_op jit(solution)/shard_map/all_to_all | solution.py:14
  28.5 0.2 stack.5
  28.7 0.0 copy-start.3
  28.8 40.7 %all_to_all.42 = bf16[32,32,1024]{2,1,0:T(8,128)(2,1)S(1)} all-to-all(bf16[32,32,1024]{2,1,0:T(8,128)(2,1)S(1)} %stack.5), channel_id=1, replica_groups=mesh['fsdp'=32,'dp'=4] {'fsdp'}, dimensions={0} | all-to-all | bytes 4194304 | tf_op jit(solution)/shard_map/all_to_all | solution.py:19
  69.5 0.0 copy-start.1
  69.5 1.3 copy-done.1
  70.8 0.0 copy-done.3
  70.8 6.6 fusion.9
  77.5 0.0 reduce-scatter.6.cloned.1.call-update
  77.5 0.0 reduce-scatter.4.cloned.1.call-start
  77.5 113.4 %all-gather.3.cloned.1.call-done = bf16[1024,2048]{1,0:T(8,128)(2,1)} async-done(((bf16[32,2048]{1,0:T(8,128)(2,1)}), bf16[1024,2048]{1,0:T(8,128)(2,1)}) %all-gather.3.cloned.1.call-update) | async-done | bytes 4194320 | tf_op jit(solution)/shard_map/all_gather | solution.py:24
  190.9 14.5 %fusion.8 = f32[1024,2048]{1,0:T(8,128)} fusion(bf16[1024,2048]{1,0:T(8,128)(2,1)} %all-gather.3.cloned.1.call-done, bf16[2048,2048]{1,0:T(8,128)(2,1)} %param.9), kind=kOutput, calls=%fused_computation.17 | convolution fusion | flops 8589934592 | bytes 20971520 | tf_op jit(solution)/shard_map/dot_general | solution.py:29
  205.4 0.0 reduce-scatter.4.cloned.1.call-update
  205.4 0.0 all-gather.5.cloned.1.call-start
  205.5 0.8 dynamic_slice.11
  206.2 0.0 reduce-scatter.6.cloned.1.call-done
  206.2 0.0 copy-start
  206.3 1.9 reduce_max.19
  208.2 73.8 %reduce-scatter.4.cloned.1.call-done = f32[256,2048]{1,0:T(8,128)} async-done(((f32[1024,2048]{1,0:T(8,128)}), f32[256,2048]{1,0:T(8,128)}) %reduce-scatter.4.cloned.1.call-update) | async-done | bytes 2097168 | tf_op jit(solution)/shard_map/reduce_scatter | solution.py:32
  282.0 1.8 reduce_max.18
  283.7 81.8 %all-reduce.1 = (f32[256]{0:T(256)S(1)}, f32[256]{0:T(256)S(1)}) all-reduce(f32[256]{0:T(256)S(1)} %reduce_max.18, f32[256]{0:T(256)S(1)} %reduce_max.19), channel_id=1, replica_groups=mesh['fsdp'=32,'dp'=4] {'fsdp'}, use_global_device_ids=true, to_apply=%region_2.0 | all-reduce | flops 512 | bytes 4096 | tf_op jit(solution)/shard_map/pmax | solution.py:43
  365.5 0.0 copy-done
  365.5 2.8 multiply_reduce_fusion
  368.3 76.8 %all-reduce = (f32[256]{0:T(256)S(1)}, f32[256]{0:T(256)S(1)}, f32[256]{0:T(256)S(1)}, f32[256]{0:T(256)S(1)}) all-reduce(f32[256]{0:T(256)S(1)} %get-tuple-element.8, f32[256]{0:T(256)S(1)} %get-tuple-element.9, f32[256]{0:T(256)S(1)} %get-tuple-element.7, f32[256]{0:T(256)S(1)} %get-tuple-element.6), channel_id=1, replica_groups=mesh['fsdp'=32,'dp'=4] {'fsdp'}, use_global_device_ids=true, to_apply=%region_13.0 | all-reduce | flops 1024 | bytes 8192 | tf_op jit(solution)/shard_map/psum | solution.py:48
  445.2 1.3 subtract_multiply_fusion
  446.5 3.4 fusion.5
  450.0 0.0 all-gather.5.cloned.1.call-update
  450.0 0.2 reduce-scatter.8.cloned.1.call-start
  450.2 35.0 %all-gather.5.cloned.1.call-done = bf16[1024,2048]{1,0:T(8,128)(2,1)} async-done(((bf16[256,2048]{1,0:T(8,128)(2,1)}), bf16[1024,2048]{1,0:T(8,128)(2,1)}) %all-gather.5.cloned.1.call-update) | async-done | bytes 4194320 | tf_op jit(solution)/shard_map/all_gather | solution.py:68
  485.2 10.0 %fusion.10 = f32[1024,1024]{1,0:T(8,128)} fusion(bf16[1024,2048]{1,0:T(8,128)(2,1)} %all-gather.5.cloned.1.call-done, bf16[1024,2048]{1,0:T(8,128)(2,1)} %param.10), kind=kOutput, calls=%fused_computation.19 | convolution fusion | flops 4294967296 | bytes 12582912 | tf_op jit(solution)/shard_map/dot_general | solution.py:73
  495.2 0.0 copy-start.2
  495.2 0.0 reduce-scatter.8.cloned.1.call-update
  495.2 1.6 copy-done.2
  496.7 9.0 %convolution_bitcast_fusion = f32[1024,2048]{0,1:T(8,128)} fusion(bf16[1024,2048]{1,0:T(8,128)(2,1)} %all-gather.5.cloned.1.call-done, bf16[1024,1024]{1,0:T(8,128)(2,1)S(1)} %bitcast.20), kind=kOutput, calls=%fused_computation | convolution fusion | flops 4294967296 | bytes 14680064 | tf_op jit(solution)/shard_map/dot_general | solution.py:69
  505.8 9.1 %copy.10 = f32[1024,2048]{1,0:T(8,128)} copy(f32[1024,2048]{0,1:T(8,128)} %convolution_bitcast_fusion) | data formatting | bytes 16777216
  514.9 149.0 %reduce-scatter.8.cloned.1.call-done = f32[32,1024]{1,0:T(8,128)} async-done(((f32[1024,1024]{1,0:T(8,128)}), f32[32,1024]{1,0:T(8,128)}) %reduce-scatter.8.cloned.1.call-update) | async-done | bytes 131088 | tf_op jit(solution)/shard_map/reduce_scatter | solution.py:72
  663.9 1.5 convert_element_type.15
  (1 shorter events, 0.0 us)
Async XLA Ops:
  8.0 182.9 %all-gather.3.cloned.1.call-start = ((), (), s32[]{:S(2)}) async-start(), calls=%async_computation.6 | async-start | bytes 4325376 | tf_op jit(solution)/shard_map/all_gather | solution.py:24
  19.5 186.7 %reduce-scatter.6.cloned.1.call-start = ((), (), s32[]{:S(2)}) async-start(), calls=%async_computation.8 | async-start | bytes 10485760 | tf_op jit(solution)/shard_map/reduce_scatter | solution.py:33
  28.7 42.1 %copy-start.3 = (bf16[1024,2048]{1,0:T(8,128)(2,1)S(1)}, bf16[1024,2048]{1,0:T(8,128)(2,1)}, u32[]{:S(2)}) copy-start(bf16[1024,2048]{1,0:T(8,128)(2,1)} %param.10) | copy-start | bytes 12582916
  69.5 1.4 copy-start.1
  77.5 204.5 %reduce-scatter.4.cloned.1.call-start = ((), (), s32[]{:S(2)}) async-start(), calls=%async_computation.7 | async-start | bytes 10485760 | tf_op jit(solution)/shard_map/reduce_scatter | solution.py:32
  205.4 279.8 %all-gather.5.cloned.1.call-start = ((), (), s32[]{:S(2)}) async-start(), calls=%async_computation.9 | async-start | bytes 5242880 | tf_op jit(solution)/shard_map/all_gather | solution.py:68
  206.2 159.2 %copy-start = (f32[256,2048]{1,0:T(8,128)S(1)}, f32[256,2048]{1,0:T(8,128)}, u32[]{:S(2)}) copy-start(f32[256,2048]{1,0:T(8,128)} %reduce-scatter.6.cloned.1.call-done) | copy-start | bytes 6291460
  450.0 213.9 %reduce-scatter.8.cloned.1.call-start = ((), (), s32[]{:S(2)}) async-start(), calls=%async_computation.10 | async-start | bytes 4325376 | tf_op jit(solution)/shard_map/reduce_scatter | solution.py:72
  495.2 1.6 copy-start.2
Sparse Core Ops, SparseCore 0:
  19.7 171.2 all-gather.2
  495.3 168.5 reduce-scatter.7
Sparse Core Ops, SparseCore 1:
  77.6 96.1 reduce-scatter.5
  205.5 76.4 reduce-scatter.3
  450.1 35.1 all-gather.4
